TPU v7x, 128 devices: a whole 4x4x4 slice. The times are simulated.
128 devices in a mesh: pipe: 2 (over core), tensor: 2 (over x_lo), dp: 32 (over y, z, x_hi).
Axes of the slice: x: 4 (x_hi: 2, x_lo: 2; x = x_hi * 2 + x_lo), y: 4, z: 4, core: 2. Of those that a mesh axis runs over, the one named last changes fastest.
Arguments:
- section_in: bfloat16 [2, 32, 2, 128, 1024], P('pipe', 'dp', 'tensor'), may hold values from -12 to 12
- lengths: int32 [32, 2], P('dp'), may hold values from 32 to 128, as said below
- qkv_weight: bfloat16 [2, 3, 1024, 1024], P('pipe', None, None, 'tensor'), may hold values from -0.75 to 0.75
- qv_bias: bfloat16 [2, 2, 1024], P('pipe', None, 'tensor'), may hold values from -3 to 3
- out_weight: bfloat16 [2, 1024, 1024], P('pipe', 'tensor'), may hold values from -0.5 to 0.5
- up_weight: bfloat16 [2, 1024, 2048], P('pipe', None, 'tensor'), may hold values from -0.1875 to 0.1875
- up_bias: bfloat16 [2, 2048], P('pipe', 'tensor'), may hold values from -3 to 3
- down_weight: bfloat16 [2, 2048, 1024], P('pipe', 'tensor'), may hold values from -0.125 to 0.125
- norm_gains: float32 [2, 2, 1024], P('pipe'), may hold values from 0.5 to 1.5
- row_biases: float32 [2, 4, 1024], P('pipe'), may hold values from -2 to 2
Outputs:
- section_out: float32 [2, 32, 2, 128, 1024], P('pipe', 'dp', 'tensor')
- qkv_grad: float32 [2, 3, 1024, 1024], P('pipe', None, None, 'tensor')
- qv_bias_grad: float32 [2, 2, 1024], P('pipe', None, 'tensor')
- out_grad: float32 [2, 1024, 1024], P('pipe', 'tensor')
- up_grad: float32 [2, 1024, 2048], P('pipe', None, 'tensor')
- up_bias_grad: float32 [2, 2048], P('pipe', 'tensor')
- down_grad: float32 [2, 2048, 1024], P('pipe', 'tensor')
- gain_grad: float32 [2, 2, 1024], P('pipe')
- bias_grad: float32 [2, 4, 1024], P('pipe')
Inputs may be any that keep to these rules, and one draw needn't show every extreme that they name: `lengths`: some sequence has length exactly 128 and some exactly 32.
All inputs are finite; a program needn't handle non-finite values.
Results may differ from a plain program's by a relative error of at most 0.023.
Values may be sent and summed in bfloat16 or wider, within the bound.
No kernel may reach another device: no remote copies, remote signals or barrier semaphores. Data moves between devices by JAX's collectives and lax.ppermute only.
A program may use at most 128 MiB of HBM per device.

v0:
```python
import jax
import jax.numpy as jnp
from jax import lax
from jax.sharding import PartitionSpec as P

HEADS = 16
HD = 64


norm_eps = 1e-05


def shifted(value, axis, steps):
    count = lax.axis_size(axis)
    initial, last = (max(0, -steps), min(count, count - steps))
    return lax.ppermute(value, axis, [(source, source + steps) for source in range(initial, last)])


def gelu_tanh(pre_act):
    return (
        0.5
        * pre_act
        * (1.0 + jnp.tanh(0.7978845608028654 * (pre_act + 0.044715 * pre_act * pre_act * pre_act)))
    )


def norm_fwd(values, gain, shift):
    centred = values - jnp.mean(values, axis=-1, keepdims=True)
    inv_std = lax.rsqrt(jnp.mean(centred * centred, axis=-1, keepdims=True) + norm_eps)
    normed = centred * inv_std
    return (normed * gain + shift, normed, inv_std)


def norm_back(grad_norm, normed, inv_std, gain):
    scaled = grad_norm * gain
    return inv_std * (
        scaled
        - jnp.mean(scaled, axis=-1, keepdims=True)
        - normed * jnp.mean(scaled * normed, axis=-1, keepdims=True)
    )


def rows_product(source, weight, form):
    return jnp.einsum(form, source, weight, preferred_element_type=jnp.float32)


def local(
    section_in,
    lengths,
    qkv_weight,
    qv_bias,
    out_weight,
    up_weight,
    up_bias,
    down_weight,
    norm_gains,
    row_biases,
):
    section_index = lax.axis_index("pipe")
    tensor_index = lax.axis_index("tensor")
    tensor_size = lax.axis_size("tensor")
    groups = section_in.shape[1]
    seq_len = section_in.shape[3]
    model_width = section_in.shape[4]
    total_rows = tensor_size * seq_len
    qkv_w = qkv_weight[0]
    qv_b = qv_bias[0]
    out_w = out_weight[0]
    up_w = up_weight[0]
    up_b = up_bias[0].astype(jnp.float32)
    down_w = down_weight[0]
    gains = norm_gains[0]
    shifts = row_biases[0]
    local_width = qkv_w.shape[2]
    heads_dev = local_width // HD
    head_ids = tensor_index * heads_dev + jnp.arange(heads_dev) + 1
    slopes = 2.0 ** (-8.0 * head_ids.astype(jnp.float32) / HEADS)
    offsets = (jnp.arange(seq_len)[:, None] - jnp.arange(seq_len)[None, :]).astype(jnp.float32)
    key_pos = jnp.arange(seq_len)
    bias_three = jnp.stack([qv_b[0], jnp.zeros_like(qv_b[0]), qv_b[1]]).astype(jnp.float32)[
        :, None, :
    ]
    inputs_all = section_in[0, :, 0]

    def split_heads(block):
        return block.reshape(tensor_size, seq_len, heads_dev, HD)

    def masked_scores(projected, seq_lengths):
        scores = (
            jnp.einsum(
                "bqhd,bkhd->bhqk",
                split_heads(projected[0]),
                split_heads(projected[1]),
                preferred_element_type=jnp.float32,
            )
            * 0.125
            - slopes[None, :, None, None] * offsets
        )
        allowed = (offsets >= 0)[None, None] & (
            key_pos[None, None, None, :] < seq_lengths[:, None, None, None]
        )
        return jnp.where(allowed, scores, -jnp.inf)

    def layer_forward(layer_in, seq_lengths):
        layer_wide = layer_in.astype(jnp.float32)
        attn_f, _, _ = norm_fwd(layer_wide, gains[0], shifts[0])
        attn_full = lax.all_gather(attn_f.astype(jnp.bfloat16), "tensor", axis=0, tiled=True)
        projected = (
            jnp.einsum("rd,cdw->crw", attn_full, qkv_w, preferred_element_type=jnp.float32)
            + bias_three
        ).astype(jnp.bfloat16)
        scores = masked_scores(projected, seq_lengths)
        top_score = jnp.max(scores, axis=-1, keepdims=True)
        exp_scores = jnp.exp(scores - top_score)
        totals = jnp.sum(exp_scores, axis=-1, keepdims=True)
        att_prob = (exp_scores / totals).astype(jnp.bfloat16)
        log_total = top_score + jnp.log(totals)
        context = (
            jnp.einsum(
                "bhqk,bkhd->bqhd",
                att_prob,
                split_heads(projected[2]),
                preferred_element_type=jnp.float32,
            )
            .reshape(total_rows, local_width)
            .astype(jnp.bfloat16)
        )
        attn_out = lax.psum_scatter(
            rows_product(context, out_w, "rw,wd->rd"), "tensor", scatter_dimension=0, tiled=True
        )
        residual = layer_wide + attn_out + shifts[1]
        mlp_f, _, _ = norm_fwd(residual, gains[1], shifts[2])
        mlp_full = lax.all_gather(mlp_f.astype(jnp.bfloat16), "tensor", axis=0, tiled=True)
        pre_gelu = jnp.dot(mlp_full, up_w, preferred_element_type=jnp.float32) + up_b
        activated = gelu_tanh(pre_gelu).astype(jnp.bfloat16)
        mlp_out = lax.psum_scatter(
            rows_product(activated, down_w, "rf,fd->rd"), "tensor", scatter_dimension=0, tiled=True
        )
        layer_out = residual + mlp_out + shifts[3]
        saved = (layer_in, projected, log_total, context, residual, pre_gelu, activated)
        return (layer_out, saved)

    def layer_backward(grad_out, saved, seq_lengths):
        layer_in, projected, log_total, context, residual, pre_gelu, activated = saved[:7]
        attn_f, attn_norm, attn_inv = norm_fwd(layer_in.astype(jnp.float32), gains[0], shifts[0])
        mlp_f, mlp_norm, mlp_inv = norm_fwd(residual, gains[1], shifts[2])
        mlp_full = lax.all_gather(mlp_f.astype(jnp.bfloat16), "tensor", axis=0, tiled=True)
        attn_full = lax.all_gather(attn_f.astype(jnp.bfloat16), "tensor", axis=0, tiled=True)
        grad_full = lax.all_gather(grad_out.astype(jnp.bfloat16), "tensor", axis=0, tiled=True)
        grad_down = jnp.einsum(
            "rf,rd->fd", activated, grad_full, preferred_element_type=jnp.float32
        )
        grad_act = jnp.einsum("rd,fd->rf", grad_full, down_w, preferred_element_type=jnp.float32)
        _, pull_back = jax.vjp(gelu_tanh, pre_gelu)
        grad_pre = pull_back(grad_act)[0]
        grad_pre_half = grad_pre.astype(jnp.bfloat16)
        grad_up = jnp.einsum(
            "rd,rf->df", mlp_full, grad_pre_half, preferred_element_type=jnp.float32
        )
        grad_mlp = lax.psum_scatter(
            rows_product(grad_pre_half, up_w, "rf,df->rd"),
            "tensor",
            scatter_dimension=0,
            tiled=True,
        )
        grad_resid = grad_out + norm_back(grad_mlp, mlp_norm, mlp_inv, gains[1])
        resid_full = lax.all_gather(grad_resid.astype(jnp.bfloat16), "tensor", axis=0, tiled=True)
        grad_outw = jnp.einsum("rw,rd->wd", context, resid_full, preferred_element_type=jnp.float32)
        grad_context = split_heads(
            jnp.einsum("rd,wd->rw", resid_full, out_w, preferred_element_type=jnp.float32).astype(
                jnp.bfloat16
            )
        )
        queries = split_heads(projected[0])
        keys_all = split_heads(projected[1])
        values_all = split_heads(projected[2])
        att_prob = jnp.exp(masked_scores(projected, seq_lengths) - log_total)
        grad_prob = jnp.einsum(
            "bqhd,bkhd->bhqk", grad_context, values_all, preferred_element_type=jnp.float32
        )
        grad_values = jnp.einsum(
            "bhqk,bqhd->bkhd",
            att_prob.astype(jnp.bfloat16),
            grad_context,
            preferred_element_type=jnp.float32,
        )
        row_delta = jnp.sum(att_prob * grad_prob, axis=-1, keepdims=True)
        grad_scores = (att_prob * (grad_prob - row_delta) * 0.125).astype(jnp.bfloat16)
        grad_queries = jnp.einsum(
            "bhqk,bkhd->bqhd", grad_scores, keys_all, preferred_element_type=jnp.float32
        )
        grad_keys = jnp.einsum(
            "bhqk,bqhd->bkhd", grad_scores, queries, preferred_element_type=jnp.float32
        )
        grad_proj = jnp.stack([grad_queries, grad_keys, grad_values]).reshape(
            3, total_rows, local_width
        )
        grad_bias = jnp.stack([jnp.sum(grad_proj[0], axis=0), jnp.sum(grad_proj[2], axis=0)])
        proj_half = grad_proj.astype(jnp.bfloat16)
        grad_qkv = jnp.einsum(
            "rd,crw->cdw", attn_full, proj_half, preferred_element_type=jnp.float32
        )
        grad_attn = lax.psum_scatter(
            rows_product(proj_half, qkv_w, "crw,cdw->rd"), "tensor", scatter_dimension=0, tiled=True
        )
        grad_in = grad_resid + norm_back(grad_attn, attn_norm, attn_inv, gains[0])
        grad_gains = jnp.stack(
            [jnp.sum(grad_attn * attn_norm, axis=0), jnp.sum(grad_mlp * mlp_norm, axis=0)]
        )
        grad_shifts = jnp.stack(
            [
                jnp.sum(grad_attn, axis=0),
                jnp.sum(grad_resid, axis=0),
                jnp.sum(grad_mlp, axis=0),
                jnp.sum(grad_out, axis=0),
            ]
        )
        return (
            grad_in,
            (
                grad_qkv,
                grad_bias,
                grad_outw,
                grad_up,
                jnp.sum(grad_pre, axis=0),
                grad_down,
                grad_gains,
                grad_shifts,
            ),
        )

    def forward_tick(received, tick_index):
        own_at = jnp.minimum(tick_index, groups - 1)
        batch_at = jnp.clip(tick_index - section_index, 0, groups - 1)
        own_in = lax.dynamic_index_in_dim(inputs_all, own_at, 0, keepdims=False)
        layer_in = jnp.where(section_index == 0, own_in, received)
        seq_lengths = lax.dynamic_index_in_dim(lengths, batch_at, 0, keepdims=False)
        layer_out, saved = layer_forward(layer_in, seq_lengths)
        passed = shifted(layer_out.astype(jnp.bfloat16), "pipe", 1)
        return (passed, (layer_out, saved))

    start_rows = jnp.zeros((seq_len, model_width), jnp.bfloat16)
    _, (outputs_all, saves_all) = lax.scan(forward_tick, start_rows, jnp.arange(groups + 1))
    zero_sums = (
        jnp.zeros(qkv_w.shape, jnp.float32),
        jnp.zeros(qv_b.shape, jnp.float32),
        jnp.zeros(out_w.shape, jnp.float32),
        jnp.zeros(up_w.shape, jnp.float32),
        jnp.zeros(up_b.shape, jnp.float32),
        jnp.zeros(down_w.shape, jnp.float32),
        jnp.zeros((2, model_width), jnp.float32),
        jnp.zeros((4, model_width), jnp.float32),
    )

    def backward_tick(carry, tick_index):
        received, running = carry
        source_at = jnp.clip(tick_index + 2 * section_index - 1, 0, groups)
        batch_at = jnp.clip(tick_index + section_index - 1, 0, groups - 1)
        saved = jax.tree.map(
            lambda stacked: lax.dynamic_index_in_dim(stacked, source_at, 0, keepdims=False),
            saves_all,
        )
        own_cot = lax.dynamic_index_in_dim(
            inputs_all, jnp.minimum(tick_index, groups - 1), 0, keepdims=False
        ).astype(jnp.float32)
        live_cot = jnp.where(tick_index < groups, own_cot, jnp.zeros_like(own_cot))
        grad_out = jnp.where(section_index == 1, live_cot, received.astype(jnp.float32))
        seq_lengths = lax.dynamic_index_in_dim(lengths, batch_at, 0, keepdims=False)
        grad_in, terms = layer_backward(grad_out, saved, seq_lengths)
        passed = shifted(grad_in.astype(jnp.bfloat16), "pipe", -1)
        running = tuple((total + term for total, term in zip(running, terms)))
        return ((passed, running), grad_in)

    (_, sums), grads_all = lax.scan(backward_tick, (start_rows, zero_sums), jnp.arange(groups + 1))
    weight_sums = lax.psum((sums[0], sums[1], sums[2], sums[3], sums[4], sums[5]), "dp")
    vector_sums = lax.psum((sums[6], sums[7]), ("tensor", "dp"))
    section_out = jnp.where(section_index == 0, grads_all[1:], outputs_all[1:])[None, :, None]
    return (
        section_out,
        weight_sums[0][None],
        weight_sums[1][None],
        weight_sums[2][None],
        weight_sums[3][None],
        weight_sums[4][None],
        weight_sums[5][None],
        vector_sums[0][None],
        vector_sums[1][None],
    )


def solution(mesh):
    in_specs = (
        P("pipe", "dp", "tensor", None, None),
        P("dp", None),
        P("pipe", None, None, "tensor"),
        P("pipe", None, "tensor"),
        P("pipe", "tensor", None),
        P("pipe", None, "tensor"),
        P("pipe", "tensor"),
        P("pipe", "tensor", None),
        P("pipe", None, None),
        P("pipe", None, None),
    )
    out_specs = (
        P("pipe", "dp", "tensor", None, None),
        P("pipe", None, None, "tensor"),
        P("pipe", None, "tensor"),
        P("pipe", "tensor", None),
        P("pipe", None, "tensor"),
        P("pipe", "tensor"),
        P("pipe", "tensor", None),
        P("pipe", None, None),
        P("pipe", None, None),
    )
    return jax.shard_map(local, mesh=mesh, in_specs=in_specs, out_specs=out_specs, check_vma=False)
```

profile of v0, /device:TPU:0, one launch (start us, length us, event | category | flops | bytes accessed | tf_op | source)
XLA Modules:
  0.0 1544.7 jit_solution(1438076503732215553)
XLA Ops:
  13.6 189.5 %while.63 = (s32[]{:T(128)}, bf16[128,1024]{1,0:T(8,128)(2,1)}, f32[2,128,1024]{2,1,0:T(8,128)}, bf16[2,128,1024]{2,1,0:T(8,128)(2,1)}, bf16[2,3,256,512]{3,2,1,...) while((s32[]{:T(128)}, bf16[128,1024]{1,0:T(8,128)(2,1)}, ...), condition=%wide.region_9.10_spmd.clone.clone, body=%wide.region_0.9_spmd.clone.clone.sunk | while | flops 2227026432 | bytes 96496376 | solution.py:243
  16.5 9.5 all_gather.54
  38.9 25.6 %reduce-scatter.5.cloned.1.call-done = f32[128,1024]{1,0:T(8,128)} async-done(((f32[256,1024]{1,0:T(8,128)}), f32[128,1024]{1,0:T(8,128)}) %reduce-scatter.5.cloned.1.call-update) | async-done | bytes 524304 | tf_op jit(solution)/shard_map/while/body/eval_jaxpr/reduce_scatter | solution.py:128
  67.0 8.8 all_gather.55
  83.3 20.7 %reduce-scatter.7.cloned.1.call-done = f32[128,1024]{1,0:T(8,128)} async-done(((f32[256,1024]{1,0:T(8,128)}), f32[128,1024]{1,0:T(8,128)}) %reduce-scatter.7.cloned.1.call-update) | async-done | bytes 524304 | tf_op jit(solution)/shard_map/while/body/eval_jaxpr/reduce_scatter | solution.py:136
  112.4 8.8 all_gather.54
  134.1 23.9 %reduce-scatter.5.cloned.1.call-done = f32[128,1024]{1,0:T(8,128)} async-done(((f32[256,1024]{1,0:T(8,128)}), f32[128,1024]{1,0:T(8,128)}) %reduce-scatter.5.cloned.1.call-update) | async-done | bytes 524304 | tf_op jit(solution)/shard_map/while/body/eval_jaxpr/reduce_scatter | solution.py:128
  160.5 8.8 all_gather.55
  176.8 20.7 %reduce-scatter.7.cloned.1.call-done = f32[128,1024]{1,0:T(8,128)} async-done(((f32[256,1024]{1,0:T(8,128)}), f32[128,1024]{1,0:T(8,128)}) %reduce-scatter.7.cloned.1.call-update) | async-done | bytes 524304 | tf_op jit(solution)/shard_map/while/body/eval_jaxpr/reduce_scatter | solution.py:136
  205.5 253.4 %while.64 = (s32[]{:T(128)}, bf16[128,1024]{1,0:T(8,128)(2,1)}, f32[3,1024,512]{1,2,0:T(8,128)}, f32[2,512]{1,0:T(2,128)}, f32[512,1024]{1,0:T(8,128)}, /*index=...) while((s32[]{:T(128)}, bf16[128,1024]{1,0:T(8,128)(2,1)}, ...), condition=%wide.region_31.32_spmd.clone.clone, body=%wide.region_10.31_spmd.clone.clone.sunk | while | flops 4491193856 | bytes 120951592 | solution.py:274
  209.1 7.9 all_gather.56
  216.9 4.2 fusion.236
  251.9 8.7 all_gather.57
  280.5 3.9 convolution_bitcast_fusion.4
  285.7 4.0 select_add_fusion.11
  289.8 11.6 all_gather.59
  315.1 9.0 all_gather.58
  324.2 3.7 bitcast_add_fusion.2
  332.1 9.5 all_gather.56
  341.7 4.2 fusion.236
  376.7 8.7 all_gather.57
  405.3 3.9 convolution_bitcast_fusion.4
  410.4 5.3 select_add_fusion.11
  415.9 13.3 all_gather.59
  429.2 3.5 select_add_fusion.8
  432.7 5.1 select_add_fusion.9
  442.7 9.0 all_gather.58
  451.7 6.6 bitcast_add_fusion.2
  458.9 6.6 copy.63
  466.2 104.3 %all-reduce.1 = (f32[1,2,512]{2,1,0:T(2,128)}, f32[1,1024]{1,0:T(1,128)}) all-reduce(f32[1,2,512]{2,1,0:T(2,128)S(1)} %bitcast.394, f32[1,1024]{1,0:T(1,128)S(1)} %bitcast.393), channel_id=1, replica_groups=mesh['pipe'=2,'tensor'=2,'dp'=32] {'dp'}, use_global_device_ids=true, to_apply=%region_33.34 | all-reduce | flops 2048 | bytes 16384 | tf_op jit(solution)/shard_map/psum | solution.py:275
  570.6 950.9 %all-reduce = (f32[1,2,1024]{2,1,0:T(2,128)}, f32[1,4,1024]{2,1,0:T(4,128)}) all-reduce(f32[1,2,1024]{2,1,0:T(2,128)S(1)} %bitcast.392, f32[1,4,1024]{2,1,0:T(4,128)S(1)} %bitcast.377), channel_id=1, replica_groups=mesh['pipe'=2,'tensor'=2,'dp'=32] {'tensor','dp'}, use_global_device_ids=true, to_apply=%region_38.39 | all-reduce | flops 6144 | bytes 49152 | tf_op jit(solution)/shard_map/psum | solution.py:276
  1522.3 6.3 copy.215
  (407 shorter events, 208.4 us)
Async XLA Ops:
  13.6 50.9 %reduce-scatter.5.cloned.1.call-start = ((), (), s32[]{:S(2)}) async-start(), calls=%async_computation.5 | async-start | bytes 1572864 | tf_op jit(solution)/shard_map/while/body/eval_jaxpr/reduce_scatter | solution.py:128
  13.7 12.3 copy-start.15
  13.7 12.3 copy-start.41
  38.9 65.1 %reduce-scatter.7.cloned.1.call-start = ((), (), s32[]{:S(2)}) async-start(), calls=%async_computation.6 | async-start | bytes 1572864 | tf_op jit(solution)/shard_map/while/body/eval_jaxpr/reduce_scatter | solution.py:136
  66.6 9.2 copy-start.43
  80.9 28.6 %copy-start.39 = (f32[2,2,8,128,1]{3,2,1,4,0:T(8,128)}, f32[2,2,8,128,1]{3,2,1,4,0:T(8,128)S(1)}, u32[]{:S(2)}) copy-start(f32[2,2,8,128,1]{3,2,1,4,0:T(8,128)S(1)} %bitcast_dynamic-update-slice_fusion.21) | copy-start | bytes 49156 | tf_op jit(solution)/shard_map/while
  105.1 4.4 collective-permute-start
  109.5 48.5 %reduce-scatter.5.cloned.1.call-start = ((), (), s32[]{:S(2)}) async-start(), calls=%async_computation.5 | async-start | bytes 1572864 | tf_op jit(solution)/shard_map/while/body/eval_jaxpr/reduce_scatter | solution.py:128
  109.6 11.6 copy-start.15
  109.6 11.6 copy-start.41
  134.0 63.5 %reduce-scatter.7.cloned.1.call-start = ((), (), s32[]{:S(2)}) async-start(), calls=%async_computation.6 | async-start | bytes 1572864 | tf_op jit(solution)/shard_map/while/body/eval_jaxpr/reduce_scatter | solution.py:136
  160.1 9.3 copy-start.43
  174.5 28.6 %copy-start.39 = (f32[2,2,8,128,1]{3,2,1,4,0:T(8,128)}, f32[2,2,8,128,1]{3,2,1,4,0:T(8,128)S(1)}, u32[]{:S(2)}) copy-start(f32[2,2,8,128,1]{3,2,1,4,0:T(8,128)S(1)} %bitcast_dynamic-update-slice_fusion.21) | copy-start | bytes 49156 | tf_op jit(solution)/shard_map/while
  198.6 4.4 collective-permute-start
  205.5 44.1 %copy-start.8 = (bf16[1,128,1024]{2,1,0:T(8,128)(2,1)}, bf16[1,128,1024]{2,1,0:T(8,128)(2,1)S(1)}, u32[]{:S(2)}) copy-start(bf16[1,128,1024]{2,1,0:T(8,128)(2,1)S(1)} %get-tuple-element.1786) | copy-start | bytes 786436 | tf_op jit(solution)/shard_map/while
  205.5 42.1 %reduce-scatter.9.cloned.1.call-start = ((), (), s32[]{:S(2)}) async-start(), calls=%async_computation.7 | async-start | bytes 1572864 | tf_op jit(solution)/shard_map/while/body/eval_jaxpr/reduce_scatter | solution.py:160
  223.6 86.6 %reduce-scatter.11.cloned.1.call-start = ((), (), s32[]{:S(2)}) async-start(), calls=%async_computation.8 | async-start | bytes 1572864 | tf_op jit(solution)/shard_map/while/body/eval_jaxpr/reduce_scatter | solution.py:203
  249.6 11.1 copy-start.6
  261.8 7.6 copy-start.13
  285.7 15.7 %copy-start.31 = (f32[2,512]{1,0:T(2,128)S(1)}, f32[2,512]{1,0:T(2,128)}, u32[]{:S(2)}) copy-start(f32[2,512]{1,0:T(2,128)} %get-tuple-element.1741) | copy-start | bytes 12292 | tf_op jit(solution)/shard_map/while
  313.9 14.1 collective-permute-start.1
  328.5 45.8 %copy-start.8 = (bf16[1,128,1024]{2,1,0:T(8,128)(2,1)}, bf16[1,128,1024]{2,1,0:T(8,128)(2,1)S(1)}, u32[]{:S(2)}) copy-start(bf16[1,128,1024]{2,1,0:T(8,128)(2,1)S(1)} %get-tuple-element.1786) | copy-start | bytes 786436 | tf_op jit(solution)/shard_map/while
  328.5 43.8 %reduce-scatter.9.cloned.1.call-start = ((), (), s32[]{:S(2)}) async-start(), calls=%async_computation.7 | async-start | bytes 1572864 | tf_op jit(solution)/shard_map/while/body/eval_jaxpr/reduce_scatter | solution.py:160
  348.4 89.4 %reduce-scatter.11.cloned.1.call-start = ((), (), s32[]{:S(2)}) async-start(), calls=%async_computation.8 | async-start | bytes 1572864 | tf_op jit(solution)/shard_map/while/body/eval_jaxpr/reduce_scatter | solution.py:203
  374.3 11.1 copy-start.6
  386.5 7.5 copy-start.13
  410.4 18.7 %copy-start.31 = (f32[2,512]{1,0:T(2,128)S(1)}, f32[2,512]{1,0:T(2,128)}, u32[]{:S(2)}) copy-start(f32[2,512]{1,0:T(2,128)} %get-tuple-element.1741) | copy-start | bytes 12292 | tf_op jit(solution)/shard_map/while
  441.4 17.0 %collective-permute-start.1 = (bf16[128,1024]{1,0:T(8,128)(2,1)S(1)}, bf16[128,1024]{1,0:T(8,128)(2,1)}, u32[]{:S(2)}, u32[]{:S(2)}) collective-permute-start(bf16[128,1024]{1,0:T(8,128)(2,1)S(1)} %get-tuple-element.1618), channel_id=1, source_target_pairs={{64,0},{65,1},{66,2},{67,3},{68,4},{69,5},{70,6},{71,7},{72,8},{73... | collective-permute-start | bytes 786440 | tf_op jit(solution)/shard_map/while/body/eval_jaxpr/ppermute | solution.py:16
  458.9 1063.4 %all-reduce.5.cloned.1.call-start = ((), (), s32[]{:S(2)}) async-start(), calls=%async_computation.4 | async-start | bytes 33554432 | tf_op jit(solution)/shard_map/psum | solution.py:275
  465.5 105.0 %copy-start.27 = (f32[2,1024]{1,0:T(2,128)S(1)}, f32[2,1024]{1,0:T(2,128)}, u32[]{:S(2)}) copy-start(f32[2,1024]{1,0:T(2,128)} %get-tuple-element.751) | copy-start | bytes 24580
  465.5 1055.9 %copy-start.20 = (f32[2,128,1024]{2,1,0:T(8,128)S(1)}, f32[2,128,1024]{2,1,0:T(8,128)}, u32[]{:S(2)}) copy-start(f32[2,128,1024]{2,1,0:T(8,128)} %get-tuple-element.743) | copy-start | bytes 3145732
  465.5 1055.9 %copy-start.21 = (f32[2,128,1024]{2,1,0:T(8,128)S(1)}, f32[2,128,1024]{2,1,0:T(8,128)}, u32[]{:S(2)}) copy-start(f32[2,128,1024]{2,1,0:T(8,128)} %get-tuple-element.744) | copy-start | bytes 3145732
  (59 other events, 195.8 us)
Sparse Core Ops, SparseCore 0:
  39.0 25.4 reduce-scatter.4
  80.1 23.8 reduce-scatter.6
  134.2 23.7 reduce-scatter.4
  173.7 23.8 reduce-scatter.6
  223.7 23.7 reduce-scatter.8
  284.6 25.6 reduce-scatter.10
  348.5 23.7 reduce-scatter.8
  409.3 26.9 reduce-scatter.10
Sparse Core Ops, SparseCore 1:
  465.6 743.7 all-reduce.4
where the time goes:
time: 1550 us; the launch traced here: 1540 us
  blocking collectives  1170 us (75%)
  waiting for transfers between devices  99.9 us (6%)
  local copies, waits for them, and re-layouts  99 us (6%)
  matrix products  98.1 us (6%)
  other arithmetic  51.6 us (3%)
  between operations  15.6 us (1%)
    psum x1, blocking collectives, local(): vector_sums = lax.psum((sums[6], sums[7]), ('tensor', 'dp'))  951 us
    psum x1, blocking collectives, local(): lax.psum((sums[0], sums[1], sums[2], sums[3], sums[4], sums[5]), 'dp')  104 us
    reduce_scatter x2, waiting for transfers between devices, layer_forward(): lax.psum_scatter(rows_product(context, out_w, 'rw,wd->rd'), 'tensor', sca...  49.5 us
    reduce_scatter x2, waiting for transfers between devices, layer_forward(): lax.psum_scatter(rows_product(activated, down_w, 'rf,fd->rd'), 'tensor',...  41.4 us
    squeeze x18, local copies, waits for them, and re-layouts, split_heads(): return block.reshape(tensor_size, seq_len, heads_dev, HD)  31.4 us
  transfers between devices with their start and end apart: 13, of which 7 were waited for; matrix products, arithmetic and copies ran while one was open for 6% of the time, Pallas kernels for 0%

commit v1 on v0

v1 whole, which is shorter than its diff:
```python
import jax
import jax.numpy as jnp
from jax import lax
from jax.sharding import Mesh
from jax.sharding import PartitionSpec as P

HEADS = 16
HD = 64
LEN = 128
norm_eps = 1e-05

f32 = jnp.float32
bf16 = jnp.bfloat16

SWAP = ((0, 1), (1, 0))
PAIR_E = ((0, 1), (1, 0), (2, 3), (3, 2))
PAIR_F = ((0, 3), (3, 0), (1, 2), (2, 1))
ORDERS = (
    (("y", "E"), ("y", "F"), ("z", "E"), ("z", "F"), ("xh", "X")),
    (("y", "F"), ("y", "E"), ("z", "F"), ("z", "E"), ("xh", "X")),
    (("z", "E"), ("z", "F"), ("y", "E"), ("y", "F"), ("xh", "X")),
    (("z", "F"), ("z", "E"), ("y", "F"), ("y", "E"), ("xh", "X")),
)
PAIRS = {"E": PAIR_E, "F": PAIR_F, "X": SWAP}


def gelu_tanh(pre_act):
    return (
        0.5
        * pre_act
        * (1.0 + jnp.tanh(0.7978845608028654 * (pre_act + 0.044715 * pre_act * pre_act * pre_act)))
    )


def norm_stats(values):
    centred = values - jnp.mean(values, axis=-1, keepdims=True)
    inv_std = lax.rsqrt(jnp.mean(centred * centred, axis=-1, keepdims=True) + norm_eps)
    return centred * inv_std, inv_std


def norm_back(grad_norm, normed, inv_std, gain):
    scaled = grad_norm * gain
    return inv_std * (
        scaled
        - jnp.mean(scaled, axis=-1, keepdims=True)
        - normed * jnp.mean(scaled * normed, axis=-1, keepdims=True)
    )


def dot(form, left, right):
    return jnp.einsum(form, left, right, preferred_element_type=f32)


def step_bit(axis, kind):
    index = lax.axis_index(axis)
    if kind == "E":
        return (index ^ (index >> 1)) & 1
    if kind == "F":
        return (index >> 1) & 1
    return index


def reduce_parts(parts):
    shaped = [part.reshape((2, 2, 2, 2, 2, part.shape[0] // 32, part.shape[1])) for part in parts]
    for level in range(5):
        received = []
        kept = []
        for value, order in zip(shaped, ORDERS):
            axis, kind = order[level]
            bit = step_bit(axis, kind)
            kept.append(lax.dynamic_index_in_dim(value, bit, 0, keepdims=False))
            sent = lax.dynamic_index_in_dim(value, 1 - bit, 0, keepdims=False).astype(bf16)
            received.append(lax.ppermute(sent, axis, PAIRS[kind]))
        shaped = [own + other.astype(f32) for own, other in zip(kept, received)]
    return shaped


def gather_parts(chunks, layer):
    values = [chunk[:, None] for chunk in chunks]
    for level in range(4, -1, -1):
        grown = []
        for value, order in zip(values, ORDERS):
            axis, kind = order[level]
            bit = step_bit(axis, kind)
            size = lax.axis_size(axis)
            pairs = [(layer * size + s, layer * size + d) for s, d in PAIRS[kind]]
            other = lax.ppermute(value, ("pipe", axis), pairs)
            grown.append(
                jnp.where(
                    bit == 0,
                    jnp.concatenate([value, other], axis=1),
                    jnp.concatenate([other, value], axis=1),
                )
            )
        values = grown
    return values


def local(
    section_in,
    lengths,
    qkv_weight,
    qv_bias,
    out_weight,
    up_weight,
    up_bias,
    down_weight,
    norm_gains,
    row_biases,
):
    core = lax.axis_index("pipe")
    tensor_index = lax.axis_index("tensor")
    place = core * 2 + tensor_index
    both = ("pipe", "tensor")

    own_rows = section_in[0, 0, 0]
    near = lax.ppermute(own_rows, both, ((0, 1), (1, 2)))
    far = lax.ppermute(own_rows, both, ((1, 3),))
    layer_in = jnp.where(place == 0, own_rows, jnp.where(place == 3, far, near))

    owned = (
        qkv_weight[0],
        out_weight[0],
        up_weight[0],
        down_weight[0],
        qv_bias[0],
        up_bias[0],
        norm_gains[0],
        row_biases[0],
    )
    other = tuple(lax.ppermute(array, "pipe", SWAP) for array in owned)
    layers = tuple(
        tuple(jnp.where(core == layer, mine, theirs) for mine, theirs in zip(owned, other))
        for layer in range(2)
    )
    cot_near = lax.ppermute(own_rows, both, ((2, 0), (3, 2)))
    cot_far = lax.ppermute(own_rows, both, ((2, 1),))
    cotangent = jnp.where(place == 3, own_rows, jnp.where(place == 1, cot_far, cot_near))

    seq_length = jnp.where(core == 0, lengths[0, 0], lengths[0, 1])
    heads_dev = HEADS // 2
    head_ids = tensor_index * heads_dev + jnp.arange(heads_dev) + 1
    slopes = 2.0 ** (-8.0 * head_ids.astype(f32) / HEADS)
    offsets = (jnp.arange(LEN)[:, None] - jnp.arange(LEN)[None, :]).astype(f32)
    allowed = (offsets >= 0) & (jnp.arange(LEN)[None, :] < seq_length)
    penalty = slopes[:, None, None] * offsets

    def split_heads(block):
        return block.reshape(LEN, heads_dev, HD)

    def masked_scores(projected):
        scores = (
            dot("qhd,khd->hqk", split_heads(projected[0]), split_heads(projected[1])) * 0.125
            - penalty
        )
        return jnp.where(allowed[None], scores, -jnp.inf)

    def tensor_sum(partial):
        swapped = lax.ppermute(partial.astype(bf16), "tensor", SWAP)
        return partial + swapped.astype(f32)

    def layer_forward(rows, params):
        qkv_w, out_w, up_w, down_w, qv_b, up_b, gains, shifts = params
        wide = rows.astype(f32)
        attn_norm, attn_inv = norm_stats(wide)
        attn_rows = (attn_norm * gains[0] + shifts[0]).astype(bf16)
        bias_three = jnp.stack([qv_b[0], jnp.zeros_like(qv_b[0]), qv_b[1]]).astype(f32)[:, None, :]
        projected = (dot("rd,cdw->crw", attn_rows, qkv_w) + bias_three).astype(bf16)
        scores = masked_scores(projected)
        top_score = jnp.max(scores, axis=-1, keepdims=True)
        exp_scores = jnp.exp(scores - top_score)
        totals = jnp.sum(exp_scores, axis=-1, keepdims=True)
        prob = exp_scores / totals
        context = (
            dot("hqk,khd->qhd", prob.astype(bf16), split_heads(projected[2]))
            .reshape(LEN, heads_dev * HD)
            .astype(bf16)
        )
        residual = wide + tensor_sum(dot("rw,wd->rd", context, out_w)) + shifts[1]
        mlp_norm, mlp_inv = norm_stats(residual)
        mlp_rows = (mlp_norm * gains[1] + shifts[2]).astype(bf16)
        pre_gelu = dot("rd,df->rf", mlp_rows, up_w) + up_b.astype(f32)
        activated = gelu_tanh(pre_gelu).astype(bf16)
        layer_out = residual + tensor_sum(dot("rf,fd->rd", activated, down_w)) + shifts[3]
        saved = (
            attn_norm,
            attn_inv,
            attn_rows,
            projected,
            prob,
            context,
            mlp_norm,
            mlp_inv,
            mlp_rows,
            pre_gelu,
            activated,
        )
        return layer_out, saved

    def half_of(block, which):
        width = block.shape[1] // 2
        return lax.dynamic_slice_in_dim(block, which * width, width, 1)

    def weight_grad(left, right):
        kept = half_of(left, core)
        sent = half_of(left, 1 - core)
        left_far = lax.ppermute(sent, "pipe", SWAP)
        right_far = lax.ppermute(right, "pipe", SWAP)
        form = "rx,ry->xy" if right.ndim == 2 else "rx,cry->cxy"
        return dot(form, kept, right) + dot(form, left_far, right_far)

    def layer_backward(grad_out, saved, params, layer):
        qkv_w, out_w, up_w, down_w, qv_b, up_b, gains, shifts = params
        (
            attn_norm,
            attn_inv,
            attn_rows,
            projected,
            prob,
            context,
            mlp_norm,
            mlp_inv,
            mlp_rows,
            pre_gelu,
            activated,
        ) = saved
        grad_half = grad_out.astype(bf16)
        grad_act = dot("rd,fd->rf", grad_half, down_w)
        _, pull_back = jax.vjp(gelu_tanh, pre_gelu)
        grad_pre = pull_back(grad_act)[0]
        grad_pre_half = grad_pre.astype(bf16)
        grad_mlp = tensor_sum(dot("rf,df->rd", grad_pre_half, up_w))
        grad_down = weight_grad(activated, grad_half)
        grad_up = weight_grad(mlp_rows, grad_pre_half)
        early = reduce_parts([grad_down[:256], grad_down[256:], grad_up[:256], grad_up[256:]])
        grad_resid = grad_out + norm_back(grad_mlp, mlp_norm, mlp_inv, gains[1])
        resid_half = grad_resid.astype(bf16)
        grad_context = split_heads(dot("rd,wd->rw", resid_half, out_w).astype(bf16))
        queries = split_heads(projected[0])
        keys_all = split_heads(projected[1])
        values_all = split_heads(projected[2])
        grad_prob = dot("qhd,khd->hqk", grad_context, values_all)
        grad_values = dot("hqk,qhd->khd", prob.astype(bf16), grad_context)
        row_delta = jnp.sum(prob * grad_prob, axis=-1, keepdims=True)
        grad_scores = (prob * (grad_prob - row_delta) * 0.125).astype(bf16)
        grad_queries = dot("hqk,khd->qhd", grad_scores, keys_all)
        grad_keys = dot("hqk,qhd->khd", grad_scores, queries)
        grad_proj = jnp.stack([grad_queries, grad_keys, grad_values]).reshape(
            3, LEN, heads_dev * HD
        )
        proj_half = grad_proj.astype(bf16)
        grad_attn = tensor_sum(dot("crw,cdw->rd", proj_half, qkv_w))
        grad_out_w = weight_grad(context, resid_half)
        grad_qkv = weight_grad(attn_rows, proj_half)
        late = reduce_parts([grad_qkv[0], grad_qkv[1], grad_qkv[2], grad_out_w])
        grad_in = grad_resid + norm_back(grad_attn, attn_norm, attn_inv, gains[0])
        vectors = jnp.stack(
            [
                jnp.concatenate([jnp.sum(grad_proj[0], axis=0), jnp.sum(grad_proj[2], axis=0)]),
                jnp.sum(grad_pre, axis=0),
                jnp.sum(grad_attn * attn_norm, axis=0),
                jnp.sum(grad_mlp * mlp_norm, axis=0),
                jnp.sum(grad_attn, axis=0),
                jnp.sum(grad_resid, axis=0),
                jnp.sum(grad_mlp, axis=0),
                jnp.sum(grad_out, axis=0),
            ]
        )

        def gathered(chunks):
            pairs = []
            for chunk in chunks:
                mine = chunk.astype(bf16).reshape(chunk.shape[-2:])
                theirs = lax.ppermute(mine, "pipe", ((1 - layer, layer),))
                pairs.append(jnp.stack([mine, theirs] if layer == 0 else [theirs, mine]))
            return gather_parts(pairs, layer)

        down_a, down_b, up_a, up_b_ = gathered(early)
        query_g, key_g, value_g, out_g = gathered(late)
        qkv_all = jnp.stack([query_g, key_g, value_g]).reshape(3, 1024, 512)
        out_all = out_g.reshape(512, 1024)
        up_all = jnp.stack([up_a, up_b_], axis=1).reshape(1024, 1024)
        down_all = jnp.stack([down_a, down_b], axis=1).reshape(1024, 1024)
        return grad_in, vectors, (qkv_all, out_all, up_all, down_all)

    out_zero, saved_zero = layer_forward(layer_in, layers[0])
    out_one, saved_one = layer_forward(out_zero.astype(bf16), layers[1])
    grad_one, vectors_one, weights_one = layer_backward(
        cotangent.astype(f32), saved_one, layers[1], 1
    )
    grad_zero, vectors_zero, weights_zero = layer_backward(
        grad_one.astype(bf16).astype(f32), saved_zero, layers[0], 0
    )

    first = core == 0
    swapped = lax.ppermute(jnp.where(first, vectors_one, vectors_zero), "pipe", SWAP)
    vectors = jnp.where(first, vectors_zero, vectors_one) + swapped
    for axis, kind in ORDERS[0]:
        vectors = vectors + lax.ppermute(vectors, axis, PAIRS[kind])
    shared = vectors[2:]
    shared = 0.5 * (shared + lax.ppermute(shared, "tensor", SWAP))

    crossing = lax.ppermute(jnp.where(first, out_one, grad_zero), both, ((0, 2), (3, 1)))
    kept_rows = jnp.where(first, grad_zero, out_one)
    section_out = jnp.where(core == tensor_index, kept_rows, crossing)
    qkv_g, out_g, up_g, down_g = (
        jnp.where(first, zero, one).astype(f32) for zero, one in zip(weights_zero, weights_one)
    )
    return (
        section_out[None, None, None],
        qkv_g[None],
        vectors[0].reshape(1, 2, 512),
        out_g[None],
        up_g[None],
        vectors[1][None],
        down_g[None],
        shared[:2][None],
        shared[2:][None],
    )


def solution(mesh):
    fine = Mesh(mesh.devices.reshape(2, 2, 4, 4, 2), ("pipe", "tensor", "y", "z", "xh"))
    dp = ("y", "z", "xh")
    in_specs = (
        P("pipe", dp, "tensor", None, None),
        P(dp, None),
        P("pipe", None, None, "tensor"),
        P("pipe", None, "tensor"),
        P("pipe", "tensor", None),
        P("pipe", None, "tensor"),
        P("pipe", "tensor"),
        P("pipe", "tensor", None),
        P("pipe", None, None),
        P("pipe", None, None),
    )
    out_specs = (
        P("pipe", dp, "tensor", None, None),
        P("pipe", None, None, "tensor"),
        P("pipe", None, "tensor"),
        P("pipe", "tensor", None),
        P("pipe", None, "tensor"),
        P("pipe", "tensor"),
        P("pipe", "tensor", None),
        P("pipe", None, None),
        P("pipe", None, None),
    )
    return jax.shard_map(local, mesh=fine, in_specs=in_specs, out_specs=out_specs, check_vma=False)
```

time: 1550 us -> 942 us (0.61)
  blocking collectives: 1170 us -> 0 us
  starting transfers between devices: 7.7 us -> 418 us
  waiting for transfers between devices: 99.9 us -> 309 us
  local copies, waits for them, and re-layouts: 99 us -> 57.6 us
  matrix products: 98.1 us -> 82.3 us
    psum x2 -> x0, blocking collectives: 1060 us -> none  [the longest x1 951 us: local(): vector_sums = lax.psum((sums[6], sums[7]), ('tensor', 'dp'))]
    ppermute x4 -> x220, starting transfers between devices: 7.45 us -> 418 us  [the longest x80 170 us: gather_parts(): other = lax.ppermute(value, ('pipe', axis), pairs)]
    ppermute x4 -> x220, waiting for transfers between devices: 0.01 us -> 309 us  [the longest x80 197 us: reduce_parts(): received.append(lax.ppermute(sent, axis, PAIRS[kind]))]
    all_gather x12 -> x0, blocking collectives: 114 us -> none  [the longest x2 24.9 us: layer_backward(): lax.all_gather(mlp_f.astype(jnp.bfloat16), 'tensor', axis=0, tiled=True)]
    reduce_scatter x8 -> x0, waiting for transfers between devices: 99.8 us -> none  [the longest x2 49.5 us: layer_forward(): lax.psum_scatter(rows_product(context, out_w, 'rw,wd->rd'), 'tensor', sca...]
    squeeze x18 -> x0, local copies, waits for them, and re-layouts: 31.4 us -> none  [split_heads(): return block.reshape(tensor_size, seq_len, heads_dev, HD)]
    convert_element_type x4 -> x85, local copies, waits for them, and re-layouts: 0.88 us -> 27.3 us  [the longest x80 21 us: reduce_parts(): lax.dynamic_index_in_dim(value, 1 - bit, 0, keepdims=False).astype(bf16)]
    while x137 -> x0, local copies, waits for them, and re-layouts: 20.2 us -> none
  transfers between devices with their start and end apart: 13 -> 220, of which waited for: 7 -> 123; matrix products, arithmetic and copies ran while one was open for 6% -> 20% of each run, Pallas kernels for 0% -> 0%
where the time goes in v1:
time: 942 us; the launch traced here: 929 us
  starting transfers between devices  418 us (44%)
  waiting for transfers between devices  309 us (33%)
  matrix products  82.3 us (9%)
  local copies, waits for them, and re-layouts  57.6 us (6%)
  other arithmetic  55.2 us (6%)
    ppermute x80, waiting for transfers between devices, reduce_parts(): received.append(lax.ppermute(sent, axis, PAIRS[kind]))  197 us
    ppermute x80, starting transfers between devices, gather_parts(): other = lax.ppermute(value, ('pipe', axis), pairs)  170 us
    ppermute x80, starting transfers between devices, reduce_parts(): received.append(lax.ppermute(sent, axis, PAIRS[kind]))  141 us
    dot_general x42, matrix products, dot(): return jnp.einsum(form, left, right, preferred_element_type=f32)  80 us
    ppermute x80, waiting for transfers between devices, gather_parts(): other = lax.ppermute(value, ('pipe', axis), pairs)  56.5 us
    ppermute x16, starting transfers between devices, gathered(): theirs = lax.ppermute(mine, 'pipe', ((1 - layer, layer),))  36.6 us
    ppermute x8, starting transfers between devices, tensor_sum(): swapped = lax.ppermute(partial.astype(bf16), 'tensor', SWAP)  35.6 us
    convert_element_type x80, local copies, waits for them, and re-layouts, reduce_parts(): lax.dynamic_index_in_dim(value, 1 - bit, 0, keepdims=False).astype(bf16)  21 us
  transfers between devices with their start and end apart: 220, of which 123 were waited for; matrix products, arithmetic and copies ran while one was open for 20% of the time, Pallas kernels for 0%

profile of v1, /device:TPU:0, one launch (start us, length us, event | category | flops | bytes accessed | tf_op | source)
XLA Modules:
  0.0 928.9 jit_solution(16657009740023477178)
XLA Ops:
  15.3 5.5 collective-permute-start.3
  39.9 4.6 collective-permute-done.9
  68.0 4.3 collective-permute-done.14
  213.9 4.5 collective-permute-done.162
  244.3 13.6 %collective-permute-start.165 = (bf16[8,1024]{1,0:T(8,128)(2,1)S(1)}, bf16[8,1024]{1,0:T(8,128)(2,1)S(1)}, u32[]{:S(2)}, u32[]{:S(2)}) collective-permute-start(bf16[8,1024]{1,0:T(8,128)(2,1)S(1)} %fusion.217), channel_id=1, source_target_pairs={{0,64},{1,65},{2,66},{3,67},{4,68},{5,69},{6,70},{7,71},{8,72},{9,... | collective-permute-start | bytes 49160 | tf_op jit(solution)/shard_map/ppermute | solution.py:274
  301.6 29.1 %collective-permute-start.19 = (bf16[128,1024]{1,0:T(8,128)(2,1)}, bf16[128,1024]{1,0:T(8,128)(2,1)}, u32[]{:S(2)}, u32[]{:S(2)}) collective-permute-start(bf16[128,1024]{1,0:T(8,128)(2,1)} %get-tuple-element.121), channel_id=1, source_target_pairs={{0,32},{32,0},{1,33},{33,1},{2,34},{34,2},{3,35},{35,3},{4,36},{36... | collective-permute-start | bytes 786440 | tf_op jit(solution)/shard_map/ppermute | solution.py:159
  341.3 5.8 collective-permute-done.58
  348.1 4.5 collective-permute-done.114
  399.8 5.6 collective-permute-done.59
  409.1 7.5 collective-permute-start.91
  417.6 4.3 collective-permute-done.82
  421.9 5.5 collective-permute-done.71
  530.3 7.8 collective-permute-start.218
  553.1 21.0 %collective-permute-start.187 = (bf16[2,8,1024]{2,1,0:T(8,128)(2,1)S(1)}, bf16[2,8,1024]{2,1,0:T(8,128)(2,1)S(1)}, u32[]{:S(2)}, u32[]{:S(2)}) collective-permute-start(bf16[2,8,1024]{2,1,0:T(8,128)(2,1)S(1)} %copy-done.134), channel_id=1, source_target_pairs={{0,2},{2,0},{4,6},{6,4},{1,3},{3,1},{5,7},{7,5},{8,10},{10,8},{12,... | collective-permute-start | bytes 98312 | tf_op jit(solution)/shard_map/ppermute | solution.py:73
  616.4 5.0 collective-permute-start.142
  623.8 4.9 collective-permute-start.131
  631.1 4.9 collective-permute-start.190
  638.4 4.9 collective-permute-start.179
  652.3 4.7 collective-permute-done.143
  658.9 5.4 collective-permute-done.132
  670.5 4.3 collective-permute-start.180
  678.9 4.9 collective-permute-done.100
  699.4 4.3 collective-permute-start.192
  713.3 4.9 collective-permute-done.181
  737.2 5.1 collective-permute-done.24
  742.3 4.9 collective-permute-start.105
  768.1 4.8 collective-permute-start.134
  788.8 4.7 collective-permute-done.26
  818.4 5.3 collective-permute-start.51
  825.7 5.3 collective-permute-start.40
  833.0 5.3 collective-permute-start.29
  878.6 4.8 collective-permute-start.146
  (1176 shorter events, 709.6 us)
Async XLA Ops:
  22.7 26.3 %collective-permute-start.12 = (bf16[1024,1024]{1,0:T(8,128)(2,1)}, bf16[1024,1024]{1,0:T(8,128)(2,1)}, u32[]{:S(2)}, u32[]{:S(2)}) collective-permute-start(bf16[1024,1024]{1,0:T(8,128)(2,1)} %bitcast.768), channel_id=1, source_target_pairs={{0,64},{64,0},{1,65},{65,1},{2,66},{66,2},{3,67},{67,3},{4,68},{68... | collective-permute-start | bytes 6291464 | tf_op jit(solution)/shard_map/ppermute | solution.py:131
  50.8 424.9 %collective-permute-start.22 = (bf16[128,512]{1,0:T(8,128)(2,1)}, bf16[128,512]{1,0:T(8,128)(2,1)}, u32[]{:S(2)}, u32[]{:S(2)}) collective-permute-start(bf16[128,512]{1,0:T(8,128)(2,1)} %constant_dynamic-slice_fusion.39), channel_id=1, source_target_pairs={{0,64},{64,0},{1,65},{65,1},{2,66},{66,2},{3,67},{67,3},{4,68},{68... | collective-permute-start | bytes 393224 | tf_op jit(solution)/shard_map/ppermute | solution.py:207
  53.8 34.7 %collective-permute-start.196 = (bf16[128,1024]{1,0:T(8,128)(2,1)}, bf16[128,1024]{1,0:T(8,128)(2,1)}, u32[]{:S(2)}, u32[]{:S(2)}) collective-permute-start(bf16[128,1024]{1,0:T(8,128)(2,1)} %get-tuple-element.30), channel_id=1, source_target_pairs={{0,64},{64,0},{1,65},{65,1},{2,66},{66,2},{3,67},{67,3},{4,68},{68... | collective-permute-start | bytes 786440 | tf_op jit(solution)/shard_map/ppermute | solution.py:208
  54.5 338.0 %collective-permute-start.97 = (bf16[128,256]{0,1:T(8,128)(2,1)}, bf16[128,256]{0,1:T(8,128)(2,1)}, u32[]{:S(2)}, u32[]{:S(2)}) collective-permute-start(bf16[128,256]{0,1:T(8,128)(2,1)} %constant_dynamic-slice_fusion.25), channel_id=1, source_target_pairs={{0,64},{64,0},{1,65},{65,1},{2,66},{66,2},{3,67},{67,3},{4,68},{68... | collective-permute-start | bytes 196616 | tf_op jit(solution)/shard_map/ppermute | solution.py:207
  67.2 131.9 %collective-permute-start.57 = (bf16[128,512]{1,0:T(8,128)(2,1)}, bf16[128,512]{1,0:T(8,128)(2,1)}, u32[]{:S(2)}, u32[]{:S(2)}) collective-permute-start(bf16[128,512]{1,0:T(8,128)(2,1)} %constant_dynamic-slice_fusion.32), channel_id=1, source_target_pairs={{0,64},{64,0},{1,65},{65,1},{2,66},{66,2},{3,67},{67,3},{4,68},{68... | collective-permute-start | bytes 393224 | tf_op jit(solution)/shard_map/ppermute | solution.py:207
  156.0 44.0 %collective-permute-start.56 = (bf16[3,128,512]{2,1,0:T(8,128)(2,1)}, bf16[3,128,512]{2,1,0:T(8,128)(2,1)}, u32[]{:S(2)}, u32[]{:S(2)}) collective-permute-start(bf16[3,128,512]{2,1,0:T(8,128)(2,1)} %pad_maximum_fusion), channel_id=1, source_target_pairs={{0,64},{64,0},{1,65},{65,1},{2,66},{66,2},{3,67},{67,3},{4,68},{68... | collective-permute-start | bytes 1179656 | tf_op jit(solution)/shard_map/ppermute | solution.py:208
  198.8 78.2 %collective-permute-start.123 = (bf16[128,512]{1,0:T(8,128)(2,1)}, bf16[128,512]{1,0:T(8,128)(2,1)}, u32[]{:S(2)}, u32[]{:S(2)}) collective-permute-start(bf16[128,512]{1,0:T(8,128)(2,1)} %constant_dynamic-slice_fusion.19), channel_id=1, source_target_pairs={{0,64},{64,0},{1,65},{65,1},{2,66},{66,2},{3,67},{67,3},{4,68},{68... | collective-permute-start | bytes 393224 | tf_op jit(solution)/shard_map/ppermute | solution.py:207
  199.1 63.6 %collective-permute-start.17 = (bf16[128,1024]{1,0:T(8,128)(2,1)S(1)}, bf16[128,1024]{1,0:T(8,128)(2,1)S(1)}, u32[]{:S(2)}, u32[]{:S(2)}) collective-permute-start(bf16[128,1024]{1,0:T(8,128)(2,1)S(1)} %copy-done.115), channel_id=1, source_target_pairs={{0,32},{32,0},{1,33},{33,1},{2,34},{34,2},{3,35},{35,3},{4,36},{36... | collective-permute-start | bytes 786440 | tf_op jit(solution)/shard_map/ppermute | solution.py:159
  261.8 29.9 %collective-permute-start.171 = (bf16[128,512]{1,0:T(8,128)(2,1)}, bf16[128,512]{1,0:T(8,128)(2,1)}, u32[]{:S(2)}, u32[]{:S(2)}) collective-permute-start(bf16[128,512]{1,0:T(8,128)(2,1)} %constant_dynamic-slice_fusion.9), channel_id=1, source_target_pairs={{0,64},{64,0},{1,65},{65,1},{2,66},{66,2},{3,67},{67,3},{4,68},{68... | collective-permute-start | bytes 393224 | tf_op jit(solution)/shard_map/ppermute | solution.py:207
  287.2 47.4 %collective-permute-start.80 = (bf16[2,2,2,2,16,512]{5,4,3,2,1,0:T(8,128)(2,1)}, bf16[2,2,2,2,16,512]{5,4,3,2,1,0:T(8,128)(2,1)}, u32[]{:S(2)}, u32[]{:S(2)}) collective-permute-start(bf16[2,2,2,2,16,512]{5,4,3,2,1,0:T(8,128)(2,1)} %fusion.91), channel_id=1, source_target_pairs={{0,2},{2,0},{4,6},{6,4},{1,3},{3,1},{5,7},{7,5},{8,10},{10,8},{12,... | collective-permute-start | bytes 786440 | tf_op jit(solution)/shard_map/ppermute | solution.py:73
  300.8 30.6 %collective-permute-start.205 = (bf16[2,4,8,1024]{3,2,0,1:T(8,128)(2,1)S(1)}, bf16[2,4,8,1024]{3,2,0,1:T(8,128)(2,1)S(1)}, u32[]{:S(2)}, u32[]{:S(2)}) collective-permute-start(bf16[2,4,8,1024]{3,2,0,1:T(8,128)(2,1)S(1)} %copy-done.91), channel_id=1, source_target_pairs={{64,66},{66,64},{68,70},{70,68},{65,67},{67,65},{69,71},{71,69},{7... | collective-permute-start | bytes 393224 | tf_op jit(solution)/shard_map/ppermute | solution.py:87
  301.6 104.6 %collective-permute-start.19 = (bf16[128,1024]{1,0:T(8,128)(2,1)}, bf16[128,1024]{1,0:T(8,128)(2,1)}, u32[]{:S(2)}, u32[]{:S(2)}) collective-permute-start(bf16[128,1024]{1,0:T(8,128)(2,1)} %get-tuple-element.121), channel_id=1, source_target_pairs={{0,32},{32,0},{1,33},{33,1},{2,34},{34,2},{3,35},{35,3},{4,36},{36... | collective-permute-start | bytes 786440 | tf_op jit(solution)/shard_map/ppermute | solution.py:159
  392.2 83.7 %collective-permute-start.21 = (bf16[3,128,512]{2,1,0:T(8,128)(2,1)S(1)}, bf16[3,128,512]{2,1,0:T(8,128)(2,1)S(1)}, u32[]{:S(2)}, u32[]{:S(2)}) collective-permute-start(bf16[3,128,512]{2,1,0:T(8,128)(2,1)S(1)} %copy-done.102), channel_id=1, source_target_pairs={{0,64},{64,0},{1,65},{65,1},{2,66},{66,2},{3,67},{67,3},{4,68},{68... | collective-permute-start | bytes 1179656 | tf_op jit(solution)/shard_map/ppermute | solution.py:208
  392.5 44.4 %collective-permute-start.217 = (bf16[2,8,8,1024]{3,2,0,1:T(8,128)(2,1)S(1)}, bf16[2,8,8,1024]{3,2,0,1:T(8,128)(2,1)S(1)}, u32[]{:S(2)}, u32[]{:S(2)}) collective-permute-start(bf16[2,8,8,1024]{3,2,0,1:T(8,128)(2,1)S(1)} %copy-done.75), channel_id=1, source_target_pairs={{64,72},{72,64},{80,88},{88,80},{65,73},{73,65},{81,89},{89,81},{6... | collective-permute-start | bytes 786440 | tf_op jit(solution)/shard_map/ppermute | solution.py:87
  405.4 33.1 %collective-permute-start.206 = (bf16[2,8,8,1024]{3,2,0,1:T(8,128)(2,1)S(1)}, bf16[2,8,8,1024]{3,2,0,1:T(8,128)(2,1)S(1)}, u32[]{:S(2)}, u32[]{:S(2)}) collective-permute-start(bf16[2,8,8,1024]{3,2,0,1:T(8,128)(2,1)S(1)} %copy-done.76), channel_id=1, source_target_pairs={{64,88},{88,64},{72,80},{80,72},{65,89},{89,65},{73,81},{81,73},{6... | collective-permute-start | bytes 786440 | tf_op jit(solution)/shard_map/ppermute | solution.py:87
  435.5 94.7 %collective-permute-start.169 = (bf16[2,8,8,1024]{3,2,0,1:T(8,128)(2,1)}, bf16[2,8,8,1024]{3,2,0,1:T(8,128)(2,1)}, u32[]{:S(2)}, u32[]{:S(2)}) collective-permute-start(bf16[2,8,8,1024]{3,2,0,1:T(8,128)(2,1)} %maximum_select_fusion.52), channel_id=1, source_target_pairs={{64,66},{66,64},{68,70},{70,68},{65,67},{67,65},{69,71},{71,69},{7... | collective-permute-start | bytes 786440 | tf_op jit(solution)/shard_map/ppermute | solution.py:87
  451.2 88.2 %collective-permute-start.158 = (bf16[2,8,8,1024]{3,2,0,1:T(8,128)(2,1)S(1)}, bf16[2,8,8,1024]{3,2,0,1:T(8,128)(2,1)}, u32[]{:S(2)}, u32[]{:S(2)}) collective-permute-start(bf16[2,8,8,1024]{3,2,0,1:T(8,128)(2,1)S(1)} %copy-done.74), channel_id=1, source_target_pairs={{64,70},{70,64},{66,68},{68,66},{65,71},{71,65},{67,69},{69,67},{7... | collective-permute-start | bytes 786440 | tf_op jit(solution)/shard_map/ppermute | solution.py:87
  472.7 253.1 %collective-permute-start.20 = (f32[128,1024]{1,0:T(8,128)}, f32[128,1024]{1,0:T(8,128)}, u32[]{:S(2)}, u32[]{:S(2)}) collective-permute-start(f32[128,1024]{1,0:T(8,128)} %get-tuple-element.33), channel_id=1, source_target_pairs={{0,64},{96,32},{1,65},{97,33},{2,66},{98,34},{3,67},{99,35},{4,68}... | collective-permute-start | bytes 1572872 | tf_op jit(solution)/shard_map/ppermute | solution.py:303
  496.8 119.5 %collective-permute-start.99 = (bf16[2,2,2,2,8,1024]{5,4,3,2,1,0:T(8,128)(2,1)}, bf16[2,2,2,2,8,1024]{5,4,3,2,1,0:T(8,128)(2,1)}, u32[]{:S(2)}, u32[]{:S(2)}) collective-permute-start(bf16[2,2,2,2,8,1024]{5,4,3,2,1,0:T(8,128)(2,1)} %fusion.92), channel_id=1, source_target_pairs={{0,6},{6,0},{2,4},{4,2},{1,7},{7,1},{3,5},{5,3},{8,14},{14,8},{10,... | collective-permute-start | bytes 786440 | tf_op jit(solution)/shard_map/ppermute | solution.py:73
  530.3 234.0 %collective-permute-start.218 = (bf16[2,16,8,1024]{3,2,0,1:T(8,128)(2,1)}, bf16[2,16,8,1024]{3,2,0,1:T(8,128)(2,1)S(1)}, u32[]{:S(2)}, u32[]{:S(2)}) collective-permute-start(bf16[2,16,8,1024]{3,2,0,1:T(8,128)(2,1)} %maximum_select_fusion.40), channel_id=1, source_target_pairs={{64,88},{88,64},{72,80},{80,72},{65,89},{89,65},{73,81},{81,73},{6... | collective-permute-start | bytes 1572872 | tf_op jit(solution)/shard_map/ppermute | solution.py:87
  539.4 138.5 %collective-permute-start.45 = (bf16[2,2,2,2,16,512]{5,4,3,2,1,0:T(8,128)(2,1)}, bf16[2,2,2,2,16,512]{5,4,3,2,1,0:T(8,128)(2,1)S(1)}, u32[]{:S(2)}, u32[]{:S(2)}) collective-permute-start(bf16[2,2,2,2,16,512]{5,4,3,2,1,0:T(8,128)(2,1)} %fusion.88), channel_id=1, source_target_pairs={{0,2},{2,0},{4,6},{6,4},{1,3},{3,1},{5,7},{7,5},{8,10},{10,8},{12,... | collective-permute-start | bytes 786440 | tf_op jit(solution)/shard_map/ppermute | solution.py:73
  615.6 30.7 %collective-permute-start.88 = (bf16[2,4,16,512]{3,2,0,1:T(8,128)(2,1)S(1)}, bf16[2,4,16,512]{3,2,0,1:T(8,128)(2,1)S(1)}, u32[]{:S(2)}, u32[]{:S(2)}) collective-permute-start(bf16[2,4,16,512]{3,2,0,1:T(8,128)(2,1)S(1)} %maximum_select_fusion.62), channel_id=1, source_target_pairs={{64,72},{72,64},{80,88},{88,80},{65,73},{73,65},{81,89},{89,81},{6... | collective-permute-start | bytes 393224 | tf_op jit(solution)/shard_map/ppermute | solution.py:87
  647.1 31.5 %collective-permute-start.34 = (bf16[2,2,2,2,16,512]{5,4,3,2,1,0:T(8,128)(2,1)S(1)}, bf16[2,2,2,2,16,512]{5,4,3,2,1,0:T(8,128)(2,1)S(1)}, u32[]{:S(2)}, u32[]{:S(2)}) collective-permute-start(bf16[2,2,2,2,16,512]{5,4,3,2,1,0:T(8,128)(2,1)S(1)} %copy-done.106), channel_id=1, source_target_pairs={{0,24},{24,0},{8,16},{16,8},{1,25},{25,1},{9,17},{17,9},{2,26},{26... | collective-permute-start | bytes 786440 | tf_op jit(solution)/shard_map/ppermute | solution.py:73
  677.9 25.8 %collective-permute-start.121 = (bf16[2,8,8,1024]{3,2,0,1:T(8,128)(2,1)S(1)}, bf16[2,8,8,1024]{3,2,0,1:T(8,128)(2,1)S(1)}, u32[]{:S(2)}, u32[]{:S(2)}) collective-permute-start(bf16[2,8,8,1024]{3,2,0,1:T(8,128)(2,1)S(1)} %maximum_select_fusion.48), channel_id=1, source_target_pairs={{64,66},{66,64},{68,70},{70,68},{65,67},{67,65},{69,71},{71,69},{7... | collective-permute-start | bytes 786440 | tf_op jit(solution)/shard_map/ppermute | solution.py:87
  695.3 69.9 %collective-permute-start.207 = (bf16[2,16,8,1024]{3,2,0,1:T(8,128)(2,1)S(1)}, bf16[2,16,8,1024]{3,2,0,1:T(8,128)(2,1)S(1)}, u32[]{:S(2)}, u32[]{:S(2)}) collective-permute-start(bf16[2,16,8,1024]{3,2,0,1:T(8,128)(2,1)S(1)} %copy-done.49), channel_id=1, source_target_pairs={{64,72},{72,64},{80,88},{88,80},{65,73},{73,65},{81,89},{89,81},{6... | collective-permute-start | bytes 1572872 | tf_op jit(solution)/shard_map/ppermute | solution.py:87
  703.7 138.6 %collective-permute-start.170 = (bf16[2,16,8,1024]{3,2,0,1:T(8,128)(2,1)S(1)}, bf16[2,16,8,1024]{3,2,0,1:T(8,128)(2,1)S(1)}, u32[]{:S(2)}, u32[]{:S(2)}) collective-permute-start(bf16[2,16,8,1024]{3,2,0,1:T(8,128)(2,1)S(1)} %maximum_select_fusion.36), channel_id=1, source_target_pairs={{64,70},{70,64},{66,68},{68,66},{65,71},{71,65},{67,69},{69,67},{7... | collective-permute-start | bytes 1572872 | tf_op jit(solution)/shard_map/ppermute | solution.py:87
  729.1 117.4 %collective-permute-start.159 = (bf16[2,16,8,1024]{3,2,0,1:T(8,128)(2,1)S(1)}, bf16[2,16,8,1024]{3,2,0,1:T(8,128)(2,1)S(1)}, u32[]{:S(2)}, u32[]{:S(2)}) collective-permute-start(bf16[2,16,8,1024]{3,2,0,1:T(8,128)(2,1)S(1)} %maximum_select_fusion.35), channel_id=1, source_target_pairs={{64,66},{66,64},{68,70},{70,68},{65,67},{67,65},{69,71},{71,69},{7... | collective-permute-start | bytes 1572872 | tf_op jit(solution)/shard_map/ppermute | solution.py:87
  766.1 81.3 %collective-permute-start.145 = (bf16[2,8,8,1024]{3,2,0,1:T(8,128)(2,1)S(1)}, bf16[2,8,8,1024]{3,2,0,1:T(8,128)(2,1)S(1)}, u32[]{:S(2)}, u32[]{:S(2)}) collective-permute-start(bf16[2,8,8,1024]{3,2,0,1:T(8,128)(2,1)S(1)} %maximum_select_fusion.50), channel_id=1, source_target_pairs={{0,2},{2,0},{4,6},{6,4},{1,3},{3,1},{5,7},{7,5},{8,10},{10,8},{12,... | collective-permute-start | bytes 786440 | tf_op jit(solution)/shard_map/ppermute | solution.py:87
  768.1 80.1 %collective-permute-start.134 = (bf16[2,8,8,1024]{3,2,0,1:T(8,128)(2,1)S(1)}, bf16[2,8,8,1024]{3,2,0,1:T(8,128)(2,1)S(1)}, u32[]{:S(2)}, u32[]{:S(2)}) collective-permute-start(bf16[2,8,8,1024]{3,2,0,1:T(8,128)(2,1)S(1)} %maximum_select_fusion.49), channel_id=1, source_target_pairs={{0,6},{6,0},{2,4},{4,2},{1,7},{7,1},{3,5},{5,3},{8,14},{14,8},{10,... | collective-permute-start | bytes 786440 | tf_op jit(solution)/shard_map/ppermute | solution.py:87
  846.5 37.0 %collective-permute-start.90 = (bf16[2,16,16,512]{3,2,0,1:T(8,128)(2,1)S(1)}, bf16[2,16,16,512]{3,2,0,1:T(8,128)(2,1)S(1)}, u32[]{:S(2)}, u32[]{:S(2)}) collective-permute-start(bf16[2,16,16,512]{3,2,0,1:T(8,128)(2,1)S(1)} %maximum_select_fusion.30), channel_id=1, source_target_pairs={{64,66},{66,64},{68,70},{70,68},{65,67},{67,65},{69,71},{71,69},{7... | collective-permute-start | bytes 1572872 | tf_op jit(solution)/shard_map/ppermute | solution.py:87
  847.4 38.6 %collective-permute-start.79 = (bf16[2,16,16,512]{3,2,0,1:T(8,128)(2,1)S(1)}, bf16[2,16,16,512]{3,2,0,1:T(8,128)(2,1)S(1)}, u32[]{:S(2)}, u32[]{:S(2)}) collective-permute-start(bf16[2,16,16,512]{3,2,0,1:T(8,128)(2,1)S(1)} %maximum_select_fusion.28), channel_id=1, source_target_pairs={{64,88},{88,64},{72,80},{80,72},{65,89},{89,65},{73,81},{81,73},{6... | collective-permute-start | bytes 1572872 | tf_op jit(solution)/shard_map/ppermute | solution.py:87
  875.2 47.5 %collective-permute-start.122 = (bf16[2,16,8,1024]{3,2,0,1:T(8,128)(2,1)S(1)}, bf16[2,16,8,1024]{3,2,0,1:T(8,128)(2,1)S(1)}, u32[]{:S(2)}, u32[]{:S(2)}) collective-permute-start(bf16[2,16,8,1024]{3,2,0,1:T(8,128)(2,1)S(1)} %maximum_select_fusion.32), channel_id=1, source_target_pairs={{64,70},{70,64},{66,68},{68,66},{65,71},{71,65},{67,69},{69,67},{7... | collective-permute-start | bytes 1572872 | tf_op jit(solution)/shard_map/ppermute | solution.py:87
  (363 other events, 3900.3 us)
